TPU v7x, 256 devices: a whole 4x4x8 slice. The times are simulated.
256 devices in a mesh: shard: 16 (over y, z_hi, core), rep: 16 (over x, z_lo).
Axes of the slice: x: 4, y: 4, z: 8 (z_hi: 2, z_lo: 4; z = z_hi * 4 + z_lo), core: 2. Of those that a mesh axis runs over, the one named last changes fastest.
Arguments:
- inputs: bfloat16 [50432, 768], P(('shard', 'rep')), may hold values from -6 to 6
- norm1_gain: float32 [768], replicated, may hold values from 0.25 to 1.75
- w_qkv: bfloat16 [768, 2304], P('shard'), may hold values from -0.21875 to 0.21875
- w_proj: bfloat16 [768, 768], P('shard'), may hold values from -0.875 to 0.875
- norm2_gain: float32 [768], replicated, may hold values from 0.25 to 1.75
- w_router: bfloat16 [768, 32], P('shard'), may hold values from -0.21875 to 0.21875
- w_expert_in: bfloat16 [2, 768, 3072], P(None, 'shard'), may hold values from -0.21875 to 0.21875
- w_expert_out: bfloat16 [2, 3072, 768], P(None, 'shard'), may hold values from -0.875 to 0.875
- expert_ids: int32 [50432, 2], P(('shard', 'rep')), may hold values from 0 to 1, all different within a row
- capacity: int32 [2], replicated, may hold values from 64 to 128, as said below
- cotangent: bfloat16 [50432, 768], P(('shard', 'rep')), may hold values from -6 to 6
Outputs:
- outputs: bfloat16 [50432, 768], P(('shard', 'rep'))
- grad_inputs: float32 [50432, 768], P(('shard', 'rep'))
- grad_norm1_gain: float32 [768], replicated
- grad_qkv: float32 [768, 2304], P('shard')
- grad_proj: float32 [768, 768], P('shard')
- grad_norm2_gain: float32 [768], replicated
- grad_router: float32 [768, 32], P('shard')
- grad_expert_in: float32 [2, 768, 3072], P(None, 'shard')
- grad_expert_out: float32 [2, 3072, 768], P(None, 'shard')
Inputs may be any that keep to these rules, and one draw needn't show every extreme that they name: Every expert's capacity is 64 to 128; some expert has exactly 128. `expert_ids`: the two experts of a token differ.
All inputs are finite; a program needn't handle non-finite values.
Results may differ from a plain program's by a relative error of at most 0.025.
Values may be sent and summed in bfloat16 or wider, within the bound.
No kernel may reach another device: no remote copies, remote signals or barrier semaphores. Data moves between devices by JAX's collectives and lax.ppermute only.
A program may use at most 128 MiB of HBM per device.

v0:
```python
import jax
import jax.numpy as jnp
from jax import lax
from jax.sharding import PartitionSpec as P

HEADS = 12
HD = 64
EXPERTS = 32
E_WIN = 2
SEQ = 197
CAP = 128
EPS = 1e-06


def layer_norm(values, gain):
    centred = values - jnp.mean(values, axis=-1, keepdims=True)
    inverse = lax.rsqrt(jnp.mean(centred * centred, axis=-1, keepdims=True) + EPS)
    normed = centred * inverse
    return (normed, inverse, (normed * gain).astype(jnp.bfloat16))


def layer_norm_back(grad_out, normed, inverse, gain):
    scaled = grad_out * gain
    grad_in = inverse * (
        scaled
        - jnp.mean(scaled, axis=-1, keepdims=True)
        - normed * jnp.mean(scaled * normed, axis=-1, keepdims=True)
    )
    return (grad_in, jnp.sum(grad_out * normed, axis=0))


def heads_view(block, images):
    return block.reshape(images, SEQ, HEADS, HD)


def attention_scores(qkv, images):
    width = HEADS * HD
    query = heads_view(qkv[:, :width], images)
    keys = heads_view(qkv[:, width : 2 * width], images)
    values = heads_view(qkv[:, 2 * width :], images)
    scores = jnp.einsum(
        "bqhd,bkhd->bhqk", query, keys, preferred_element_type=jnp.float32
    ) * HD ** (-0.5)
    return (query, keys, values, scores)


def attention_forward(qkv, images):
    query, keys, values, scores = attention_scores(qkv, images)
    logsum = jax.nn.logsumexp(scores, axis=-1, keepdims=True)
    probs = jnp.exp(scores - logsum).astype(jnp.bfloat16)
    mixed = jnp.einsum("bhqk,bkhd->bqhd", probs, values, preferred_element_type=jnp.float32).astype(
        jnp.bfloat16
    )
    return (mixed.reshape(images * SEQ, HEADS * HD), logsum)


def attention_backward(qkv, mixed, logsum, grad_mixed, images):
    query, keys, values, scores = attention_scores(qkv, images)
    probs_full = jnp.exp(scores - logsum)
    probs = probs_full.astype(jnp.bfloat16)
    grad_out = heads_view(grad_mixed, images)
    out_rows = heads_view(mixed, images)
    grad_values = jnp.einsum("bhqk,bqhd->bkhd", probs, grad_out, preferred_element_type=jnp.float32)
    grad_probs = jnp.einsum("bqhd,bkhd->bhqk", grad_out, values, preferred_element_type=jnp.float32)
    delta = jnp.sum(grad_out.astype(jnp.float32) * out_rows.astype(jnp.float32), axis=-1)
    delta = jnp.transpose(delta, (0, 2, 1))[..., None]
    grad_scores = (probs_full * (grad_probs - delta)).astype(jnp.bfloat16)
    scale = HD ** (-0.5)
    grad_query = (
        jnp.einsum("bhqk,bkhd->bqhd", grad_scores, keys, preferred_element_type=jnp.float32) * scale
    )
    grad_keys = (
        jnp.einsum("bhqk,bqhd->bkhd", grad_scores, query, preferred_element_type=jnp.float32)
        * scale
    )
    width = HEADS * HD
    rows = images * SEQ
    return jnp.concatenate(
        [
            grad_query.reshape(rows, width),
            grad_keys.reshape(rows, width),
            grad_values.reshape(rows, width),
        ],
        axis=1,
    ).astype(jnp.bfloat16)


def route_masks(expert_ids, capacity):
    count = expert_ids.shape[0]
    picked_hot = (expert_ids[:, :, None] == jnp.arange(E_WIN)[None, None, :]).astype(jnp.int32)
    ordered = jnp.transpose(picked_hot, (1, 0, 2)).reshape(2 * count, E_WIN)
    before = jnp.cumsum(ordered, axis=0) - ordered
    position = jnp.sum(before * ordered, axis=1).reshape(2, count).T
    limit = jnp.sum(picked_hot * capacity[None, None, :], axis=2)
    kept_mask = (position < limit).astype(jnp.float32)
    slot_hot = (position[:, :, None] == jnp.arange(CAP)[None, None, :]).astype(jnp.float32)
    return (
        kept_mask[:, :, None, None]
        * picked_hot.astype(jnp.float32)[:, :, :, None]
        * slot_hot[:, :, None, :]
    )


def body(
    inputs,
    norm1_gain,
    w_qkv,
    w_proj,
    norm2_gain,
    w_router,
    w_expert_in,
    w_expert_out,
    expert_ids,
    capacity,
    cotangent,
):
    high = lax.Precision.HIGHEST
    images = inputs.shape[0] // SEQ
    shard_rows = w_qkv.shape[0]
    hid_rows = w_expert_out.shape[1]
    full_qkv, full_proj, full_router = (
        lax.all_gather(w_qkv, "shard", axis=0, tiled=True),
        lax.all_gather(w_proj, "shard", axis=0, tiled=True),
        lax.all_gather(w_router, "shard", axis=0, tiled=True),
    )
    x_float = inputs.astype(jnp.float32)
    normed1, inverse1, hidden1 = layer_norm(x_float, norm1_gain)
    qkv = jnp.dot(hidden1, full_qkv, preferred_element_type=jnp.float32).astype(jnp.bfloat16)
    mixed, logsum = attention_forward(qkv, images)
    attended = x_float + jnp.dot(mixed, full_proj, preferred_element_type=jnp.float32)
    normed2, inverse2, hidden2 = layer_norm(attended, norm2_gain)
    logits = jnp.dot(hidden2, full_router, preferred_element_type=jnp.float32)
    router = jax.nn.softmax(logits, axis=-1)
    expert_hot = (expert_ids[:, :, None] == jnp.arange(EXPERTS)[None, None, :]).astype(jnp.float32)
    gate = jnp.sum(router[:, None, :] * expert_hot, axis=2)
    masks = route_masks(expert_ids, capacity)
    dispatch_float = jnp.sum(masks, axis=1)
    dispatch = dispatch_float.astype(jnp.bfloat16)
    combine = jnp.sum(masks * gate[:, :, None, None], axis=1)
    expert_rows = jnp.einsum(
        "rec,rd->ecd", dispatch, hidden2, preferred_element_type=jnp.float32
    ).astype(jnp.bfloat16)
    kept_weights = []
    pre_list = []
    activated_list = []
    eout_list = []
    for expert in range(E_WIN):
        first, second = (
            lax.all_gather(w_expert_in[expert], "shard", axis=0, tiled=True),
            lax.all_gather(w_expert_out[expert], "shard", axis=0, tiled=True),
        )
        kept_weights.append((first, second))
        pre = jnp.dot(expert_rows[expert], first, preferred_element_type=jnp.float32)
        activated = jax.nn.gelu(pre, approximate=False).astype(jnp.bfloat16)
        pre_list.append(pre)
        activated_list.append(activated)
        eout_list.append(
            jnp.dot(activated, second, preferred_element_type=jnp.float32).astype(jnp.bfloat16)
        )
    expert_out = jnp.stack(eout_list)
    eout_float = expert_out.astype(jnp.float32)
    moe = jnp.einsum("rec,ecd->rd", combine, eout_float, precision=high)
    outputs = (attended + moe).astype(jnp.bfloat16)
    grad = cotangent.astype(jnp.float32)
    matched = jnp.einsum("rd,ecd->rec", grad, eout_float, precision=high)
    grad_gate = jnp.sum(masks * matched[:, None, :, :], axis=(2, 3))
    grad_eout = jnp.einsum("rec,rd->ecd", combine, grad, precision=high).astype(jnp.bfloat16)
    back_qkv, back_proj, back_router = (full_qkv, full_proj, full_router)
    in_list = []
    out_list = []
    grad_rows_list = []
    for expert in range(E_WIN):
        first, second = kept_weights[expert]
        pre = pre_list[expert]
        grad_act = jnp.einsum(
            "cd,hd->ch", grad_eout[expert], second, preferred_element_type=jnp.float32
        )
        slope = (
            0.5 * (1.0 + jax.scipy.special.erf(pre * 0.7071067811865476))
            + pre * jnp.exp(-0.5 * pre * pre) * 0.3989422804014327
        )
        grad_pre = (grad_act * slope).astype(jnp.bfloat16)
        grad_rows_list.append(
            jnp.einsum("ch,dh->cd", grad_pre, first, preferred_element_type=jnp.float32).astype(
                jnp.bfloat16
            )
        )
        rows_here = expert_rows[expert]
        act_here = activated_list[expert]
        eout_here = grad_eout[expert]

        def in_term(start, count, rows_here=rows_here, grad_pre=grad_pre):
            return jnp.einsum("cd,ch->dh", rows_here, grad_pre, preferred_element_type=jnp.float32)

        def out_term(start, count, act_here=act_here, eout_here=eout_here):
            return jnp.einsum("ch,cd->hd", act_here, eout_here, preferred_element_type=jnp.float32)

        in_list.append(
            lax.psum_scatter(
                in_term(jnp.int32(0), shard_rows * lax.axis_size("shard")).astype(jnp.bfloat16),
                "shard",
                scatter_dimension=0,
                tiled=True,
            ).astype(jnp.float32)
        )
        out_list.append(
            lax.psum_scatter(
                out_term(jnp.int32(0), hid_rows * lax.axis_size("shard")).astype(jnp.bfloat16),
                "shard",
                scatter_dimension=0,
                tiled=True,
            ).astype(jnp.float32)
        )
    grad_rows = jnp.stack(grad_rows_list)
    grad_probs = jnp.sum(grad_gate[:, :, None] * expert_hot, axis=1)
    grad_logits = (
        router * (grad_probs - jnp.sum(router * grad_probs, axis=-1, keepdims=True))
    ).astype(jnp.bfloat16)
    grad_hidden2 = jnp.einsum(
        "rec,ecd->rd", dispatch, grad_rows, preferred_element_type=jnp.float32
    ) + jnp.einsum("re,de->rd", grad_logits, back_router, preferred_element_type=jnp.float32)
    grad_norm2, gain2 = layer_norm_back(grad_hidden2, normed2, inverse2, norm2_gain)
    grad_attended = grad + grad_norm2
    grad_branch = grad_attended.astype(jnp.bfloat16)
    grad_mixed = jnp.einsum(
        "rk,dk->rd", grad_branch, back_proj, preferred_element_type=jnp.float32
    ).astype(jnp.bfloat16)
    grad_qkv_rows = attention_backward(qkv, mixed, logsum, grad_mixed, images)
    grad_hidden1 = jnp.einsum(
        "rk,dk->rd", grad_qkv_rows, back_qkv, preferred_element_type=jnp.float32
    )
    grad_norm1, gain1 = layer_norm_back(grad_hidden1, normed1, inverse1, norm1_gain)
    grad_inputs = grad_attended + grad_norm1
    gain1_total, gain2_total = lax.psum((gain1, gain2), ("shard", "rep"))
    dense_local = lax.psum_scatter(
        jnp.concatenate(
            [
                jnp.einsum("rc,rk->ck", hidden1, grad_qkv_rows, preferred_element_type=jnp.float32),
                jnp.einsum("rc,rk->ck", mixed, grad_branch, preferred_element_type=jnp.float32),
                jnp.einsum("rc,rk->ck", hidden2, grad_logits, preferred_element_type=jnp.float32),
            ],
            axis=1,
        ).astype(jnp.bfloat16),
        "shard",
        scatter_dimension=0,
        tiled=True,
    )
    dense_total, in_total, out_total = (
        lax.psum(dense_local, "rep").astype(jnp.float32),
        lax.psum(jnp.stack(in_list).astype(jnp.bfloat16), "rep").astype(jnp.float32),
        lax.psum(jnp.stack(out_list).astype(jnp.bfloat16), "rep").astype(jnp.float32),
    )
    width = HEADS * HD
    return (
        outputs,
        grad_inputs,
        gain1_total,
        dense_total[:, : 3 * width],
        dense_total[:, 3 * width : 4 * width],
        gain2_total,
        dense_total[:, 4 * width :],
        in_total,
        out_total,
    )


def solution(mesh):
    in_specs = (
        P(("shard", "rep"), None),
        P(),
        P("shard", None),
        P("shard", None),
        P(),
        P("shard", None),
        P(None, "shard", None),
        P(None, "shard", None),
        P(("shard", "rep"), None),
        P(),
        P(("shard", "rep"), None),
    )
    out_specs = (
        P(("shard", "rep"), None),
        P(("shard", "rep"), None),
        P(),
        P("shard", None),
        P("shard", None),
        P(),
        P("shard", None),
        P(None, "shard", None),
        P(None, "shard", None),
    )
    return jax.shard_map(body, mesh=mesh, in_specs=in_specs, out_specs=out_specs, check_vma=False)
```

profile of v0, /device:TPU:24, one launch (start us, length us, event | category | flops | bytes accessed | tf_op | source)
XLA Modules:
  0.0 1204.1 jit_solution(413905897846838815)
XLA Ops:
  14.3 31.0 %all-gather.4 = bf16[16,48,32]{1,2,0:T(8,128)(2,1)S(1)} all-gather(bf16[1,48,32]{1,2,0:T(8,128)(2,1)S(1)} %bitcast.199), channel_id=1, replica_groups=mesh['shard'=16,'rep'=16] {'shard'}, dimensions={0}, use_global_device_ids=true | all-gather | bytes 52224 | tf_op jit(solution)/shard_map/all_gather | solution.py:124
  47.8 39.1 %all-gather.12.cloned.1.call-done = bf16[768,2304]{1,0:T(8,128)(2,1)} async-done(((bf16[48,2304]{1,0:T(8,128)(2,1)}), bf16[768,2304]{1,0:T(8,128)(2,1)}) %all-gather.12.cloned.1.call-update) | async-done | bytes 3538960 | tf_op jit(solution)/shard_map/all_gather | solution.py:122
  95.6 46.1 %all-gather.14.cloned.1.call-done = bf16[768,768]{1,0:T(8,128)(2,1)} async-done(((bf16[48,768]{1,0:T(8,128)(2,1)}), bf16[768,768]{1,0:T(8,128)(2,1)}) %all-gather.14.cloned.1.call-update) | async-done | bytes 1179664 | tf_op jit(solution)/shard_map/all_gather | solution.py:123
  149.7 72.3 %all-gather.20.cloned.1.call-done = bf16[1,768,3072]{2,1,0:T(8,128)(2,1)} async-done(((bf16[1,48,3072]{2,1,0:T(8,128)(2,1)}), bf16[1,768,3072]{2,1,0:T(8,128)(2,1)}) %all-gather.20.cloned.1.call-update) | async-done | bytes 4718608 | tf_op jit(solution)/shard_map/all_gather | solution.py:149
  222.0 7.7 fusion.34
  229.7 71.5 %all-gather.22.cloned.1.call-done = bf16[1,3072,768]{2,1,0:T(8,128)(2,1)} async-done(((bf16[1,192,768]{2,1,0:T(8,128)(2,1)}), bf16[1,3072,768]{2,1,0:T(8,128)(2,1)}) %all-gather.22.cloned.1.call-update) | async-done | bytes 4718608 | tf_op jit(solution)/shard_map/all_gather | solution.py:150
  301.2 4.0 fusion.73
  305.2 75.7 %all-gather.16.cloned.1.call-done = bf16[1,768,3072]{2,1,0:T(8,128)(2,1)} async-done(((bf16[1,48,3072]{2,1,0:T(8,128)(2,1)}), bf16[1,768,3072]{2,1,0:T(8,128)(2,1)}) %all-gather.16.cloned.1.call-update) | async-done | bytes 4718608 | tf_op jit(solution)/shard_map/all_gather | solution.py:149
  380.9 7.9 fusion.31
  388.8 71.3 %all-gather.18.cloned.1.call-done = bf16[1,3072,768]{2,1,0:T(8,128)(2,1)} async-done(((bf16[1,192,768]{2,1,0:T(8,128)(2,1)}), bf16[1,3072,768]{2,1,0:T(8,128)(2,1)}) %all-gather.18.cloned.1.call-update) | async-done | bytes 4718608 | tf_op jit(solution)/shard_map/all_gather | solution.py:150
  464.7 7.0 fusion.100
  477.4 4.7 convolution_convert_fusion.1
  482.3 4.8 fusion.22
  491.9 5.0 fusion.25
  503.7 4.3 fusion.82
  508.1 4.1 fusion.76
  531.7 49.8 %reduce-scatter.14.cloned.1.call-done = bf16[192,768]{1,0:T(8,128)(2,1)} async-done(((bf16[3072,768]{1,0:T(8,128)(2,1)}), bf16[192,768]{1,0:T(8,128)(2,1)}) %reduce-scatter.14.cloned.1.call-update) | async-done | bytes 294928 | tf_op jit(solution)/shard_map/reduce_scatter | solution.py:207
  581.5 109.2 %reduce-scatter.12.cloned.1.call-done = bf16[192,768]{1,0:T(8,128)(2,1)} async-done(((bf16[3072,768]{1,0:T(8,128)(2,1)}), bf16[192,768]{1,0:T(8,128)(2,1)}) %reduce-scatter.12.cloned.1.call-update) | async-done | bytes 294928 | tf_op jit(solution)/shard_map/reduce_scatter | solution.py:207
  692.6 106.6 %reduce-scatter.10.cloned.1.call-done = bf16[48,3072]{1,0:T(8,128)(2,1)} async-done(((bf16[768,3072]{1,0:T(8,128)(2,1)}), bf16[48,3072]{1,0:T(8,128)(2,1)}) %reduce-scatter.10.cloned.1.call-update) | async-done | bytes 294928 | tf_op jit(solution)/shard_map/reduce_scatter | solution.py:199
  799.3 109.0 %reduce-scatter.8.cloned.1.call-done = bf16[48,3072]{1,0:T(8,128)(2,1)} async-done(((bf16[768,3072]{1,0:T(8,128)(2,1)}), bf16[48,3072]{1,0:T(8,128)(2,1)}) %reduce-scatter.8.cloned.1.call-update) | async-done | bytes 294928 | tf_op jit(solution)/shard_map/reduce_scatter | solution.py:199
  910.2 108.5 %reduce-scatter.6.cloned.1.call-done = bf16[48,3104]{1,0:T(8,128)(2,1)} async-done(((bf16[768,3104]{1,0:T(8,128)(2,1)}), bf16[48,3104]{1,0:T(8,128)(2,1)}) %reduce-scatter.6.cloned.1.call-update) | async-done | bytes 298000 | tf_op jit(solution)/shard_map/reduce_scatter | solution.py:235
  1018.8 4.2 fusion.96
  1022.9 74.5 %all-reduce.1 = (f32[768]{0:T(1024)}, f32[768]{0:T(1024)}) all-reduce(f32[768]{0:T(1024)S(1)} %get-tuple-element.56, f32[768]{0:T(1024)S(1)} %get-tuple-element.54), channel_id=1, replica_groups=mesh['shard'=16,'rep'=16] {'shard','rep'}, use_global_device_ids=true, to_apply=%region_24.25 | all-reduce | flops 1536 | bytes 12288 | tf_op jit(solution)/shard_map/psum | solution.py:234
  1101.1 88.9 %all-reduce.5.cloned.1.call-done = (bf16[48,3104]{1,0:T(8,128)(2,1)}, bf16[2,48,3072]{2,1,0:T(8,128)(2,1)}, bf16[2,192,768]{2,1,0:T(8,128)(2,1)}) async-done(((bf16[48,3104]{1,0:T(8,128)(2,1)}, bf16[2,48,3072]{2,1,0:T(8,128)(2,1)}, bf16[2,192,768]{2,1,0:T(8,128)(2,1)}), (bf16[48,3104]{1,0:T(8,128)(2,1)}, bf16[2,48,3072]{2,1,0:T(8,128)(2,1)}, bf16[2,192,768]{2,1,0:T(8,128)(2,1)})) %all-reduce.5.cloned.1.call-update) | async-done | bytes 1477648 | tf_op jit(solution)/shard_map/psum | solution.py:249
  (219 shorter events, 81.5 us)
Async XLA Ops:
  7.2 79.7 %all-gather.12.cloned.1.call-start = ((), (), s32[]{:S(2)}) async-start(), calls=%async_computation.5 | async-start | bytes 3760128 | tf_op jit(solution)/shard_map/all_gather | solution.py:122
  7.9 133.8 %all-gather.14.cloned.1.call-start = ((), (), s32[]{:S(2)}) async-start(), calls=%async_computation.6 | async-start | bytes 1253376 | tf_op jit(solution)/shard_map/all_gather | solution.py:123
  8.7 213.3 %all-gather.20.cloned.1.call-start = ((), (), s32[]{:S(2)}) async-start(), calls=%async_computation.14 | async-start | bytes 5013504 | tf_op jit(solution)/shard_map/all_gather | solution.py:149
  10.7 290.5 %all-gather.22.cloned.1.call-start = ((), (), s32[]{:S(2)}) async-start(), calls=%async_computation.15 | async-start | bytes 5013504 | tf_op jit(solution)/shard_map/all_gather | solution.py:150
  11.6 75.2 %copy-start.45 = (f32[768]{0:T(1024)S(1)}, f32[768]{0:T(1024)}, u32[]{:S(2)}) copy-start(f32[768]{0:T(1024)} %param.12) | copy-start | bytes 9220
  11.6 369.3 %all-gather.16.cloned.1.call-start = ((), (), s32[]{:S(2)}) async-start(), calls=%async_computation.12 | async-start | bytes 5013504 | tf_op jit(solution)/shard_map/all_gather | solution.py:149
  12.2 447.9 %all-gather.18.cloned.1.call-start = ((), (), s32[]{:S(2)}) async-start(), calls=%async_computation.13 | async-start | bytes 5013504 | tf_op jit(solution)/shard_map/all_gather | solution.py:150
  12.8 568.7 %reduce-scatter.14.cloned.1.call-start = ((), (), s32[]{:S(2)}) async-start(), calls=%async_computation.11 | async-start | bytes 5013504 | tf_op jit(solution)/shard_map/reduce_scatter | solution.py:207
  46.5 43.3 %copy-start.19 = (f32[197,2,2]{2,1,0:T(2,128)}, f32[197,2,2]{2,1,0:T(2,128)S(1)}, u32[]{:S(2)}) copy-start(f32[197,2,2]{2,1,0:T(2,128)S(1)} %copy.110) | copy-start | bytes 9460
  46.6 43.2 %copy-start.46 = (f32[197]{0:T(256)}, f32[197]{0:T(256)S(1)}, u32[]{:S(2)}) copy-start(f32[197]{0:T(256)S(1)} %broadcast_multiply_fusion.5) | copy-start | bytes 2368
  46.9 42.9 %copy-start.50 = (f32[197]{0:T(256)}, f32[197]{0:T(256)S(1)}, u32[]{:S(2)}) copy-start(f32[197]{0:T(256)S(1)} %add_rsqrt_fusion.1) | copy-start | bytes 2368
  95.6 48.8 %copy-start.44 = (f32[768]{0:T(1024)S(1)}, f32[768]{0:T(1024)}, u32[]{:S(2)}) copy-start(f32[768]{0:T(1024)} %param.15) | copy-start | bytes 9220
  477.4 213.4 %reduce-scatter.12.cloned.1.call-start = ((), (), s32[]{:S(2)}) async-start(), calls=%async_computation.10 | async-start | bytes 5013504 | tf_op jit(solution)/shard_map/reduce_scatter | solution.py:207
  482.2 317.1 %reduce-scatter.10.cloned.1.call-start = ((), (), s32[]{:S(2)}) async-start(), calls=%async_computation.9 | async-start | bytes 5013504 | tf_op jit(solution)/shard_map/reduce_scatter | solution.py:199
  491.6 416.7 %reduce-scatter.8.cloned.1.call-start = ((), (), s32[]{:S(2)}) async-start(), calls=%async_computation.8 | async-start | bytes 5013504 | tf_op jit(solution)/shard_map/reduce_scatter | solution.py:199
  501.4 517.3 %reduce-scatter.6.cloned.1.call-start = ((), (), s32[]{:S(2)}) async-start(), calls=%async_computation.7 | async-start | bytes 5222400 | tf_op jit(solution)/shard_map/reduce_scatter | solution.py:235
  531.6 658.3 %all-reduce.5.cloned.1.call-start = ((), (), s32[]{:S(2)}) async-start(), calls=%async_computation.16 | async-start | bytes 2973696 | tf_op jit(solution)/shard_map/psum | solution.py:249
  692.6 326.1 %copy-start.38 = (bf16[12,64,197]{2,1,0:T(8,128)(2,1)S(1)}, bf16[12,64,197]{2,1,0:T(8,128)(2,1)}, u32[]{:S(2)}) copy-start(bf16[12,64,197]{2,1,0:T(8,128)(2,1)} %copy-done.37) | copy-start | bytes 907780
  692.6 326.1 %copy-start.40 = (bf16[12,64,197]{2,1,0:T(8,128)(2,1)S(1)}, bf16[12,64,197]{2,1,0:T(8,128)(2,1)}, u32[]{:S(2)}) copy-start(bf16[12,64,197]{2,1,0:T(8,128)(2,1)} %copy-done.39) | copy-start | bytes 907780
  692.6 326.1 %copy-start.42 = (bf16[12,64,197]{2,1,0:T(8,128)(2,1)S(1)}, bf16[12,64,197]{2,1,0:T(8,128)(2,1)}, u32[]{:S(2)}) copy-start(bf16[12,64,197]{2,1,0:T(8,128)(2,1)} %copy-done.41) | copy-start | bytes 907780
  1018.7 80.1 %copy-start.18 = (f32[197,2,128]{2,1,0:T(2,128)S(1)}, f32[197,2,128]{2,1,0:T(2,128)}, u32[]{:S(2)}) copy-start(f32[197,2,128]{2,1,0:T(2,128)} %copy-done.17) | copy-start | bytes 605188
  1018.7 80.1 %copy-start.27 = (bf16[1,128,768]{2,1,0:T(8,128)(2,1)S(1)}, bf16[1,128,768]{2,1,0:T(8,128)(2,1)}, u32[]{:S(2)}) copy-start(bf16[1,128,768]{2,1,0:T(8,128)(2,1)} %fusion.73) | copy-start | bytes 589828
  1018.8 80.1 %copy-start.29 = (bf16[1,128,768]{2,1,0:T(8,128)(2,1)S(1)}, bf16[1,128,768]{2,1,0:T(8,128)(2,1)}, u32[]{:S(2)}) copy-start(bf16[1,128,768]{2,1,0:T(8,128)(2,1)} %copy-done.28) | copy-start | bytes 589828
  1022.9 77.1 %copy-start.2 = (f32[197,768]{1,0:T(8,128)S(1)}, f32[197,768]{1,0:T(8,128)}, u32[]{:S(2)}) copy-start(f32[197,768]{1,0:T(8,128)} %copy-done) | copy-start | bytes 1815556
  (42 other events, 220.6 us)
Sparse Core Ops, SparseCore 0:
  10.7 76.0 all-gather.11
  89.5 52.1 all-gather.13
  145.0 76.9 all-gather.19
  224.6 76.5 all-gather.21
  304.3 76.5 all-gather.15
  383.5 76.5 all-gather.17
  477.5 103.9 reduce-scatter.13
  586.5 104.1 reduce-scatter.11
  695.1 104.1 reduce-scatter.9
  804.1 104.1 reduce-scatter.7
  912.8 105.8 reduce-scatter.5
  1022.5 167.3 all-reduce.4
where the time goes:
time: 1210 us; the launch traced here: 1200 us
  waiting for transfers between devices  951 us (79%)
  blocking collectives  106 us (9%)
  matrix products  81.6 us (7%)
  local copies, waits for them, and re-layouts  26.4 us (2%)
  other arithmetic  24 us (2%)
  between operations  15.4 us (1%)
    reduce_scatter x2, waiting for transfers between devices, body(): lax.psum_scatter(in_term(jnp.int32(0), shard_rows * lax.axis_size('shard'...  216 us
    reduce_scatter x2, waiting for transfers between devices, body(): lax.psum_scatter(out_term(jnp.int32(0), hid_rows * lax.axis_size('shard')...  159 us
    all_gather x2, waiting for transfers between devices, body(): lax.all_gather(w_expert_in[expert], 'shard', axis=0, tiled=True)  148 us
    all_gather x2, waiting for transfers between devices, body(): lax.all_gather(w_expert_out[expert], 'shard', axis=0, tiled=True)  143 us
    reduce_scatter x1, waiting for transfers between devices, body(): lax.psum_scatter(jnp.concatenate([jnp.einsum('rc,rk->ck', hidden1, grad_q...  108 us
    psum x1, waiting for transfers between devices, body(): lax.psum(dense_local, 'rep').astype(jnp.float32)  88.9 us
    psum x1, blocking collectives, body(): gain1_total, gain2_total = lax.psum((gain1, gain2), ('shard', 'rep'))  74.5 us
    all_gather x1, waiting for transfers between devices, body(): lax.all_gather(w_proj, 'shard', axis=0, tiled=True)  46.1 us
  transfers between devices with their start and end apart: 12, of which 12 were waited for; matrix products, arithmetic and copies ran while one was open for 9% of the time, Pallas kernels for 0%

commit v1 on v0

--- a/solution.py
+++ b/solution.py
@@ -146,7 +146,12 @@
     eout_list = []
     for expert in range(E_WIN):
         first, second = (
-            lax.all_gather(w_expert_in[expert], "shard", axis=0, tiled=True),
+            jnp.concatenate(
+                lax.all_to_all(
+                    jnp.stack([w_expert_in[expert]] * lax.axis_size("shard")), "shard", 0, 0
+                ),
+                axis=0,
+            ),
             lax.all_gather(w_expert_out[expert], "shard", axis=0, tiled=True),
         )
         kept_weights.append((first, second))

time: 1210 us -> 1180 us (0.975)
  waiting for transfers between devices: 951 us -> 789 us
  blocking collectives: 106 us -> 202 us
  starting transfers between devices: 0.69 us -> 27.8 us
    all_gather x2 -> x0, waiting for transfers between devices: 148 us -> none  [body(): lax.all_gather(w_expert_in[expert], 'shard', axis=0, tiled=True)]
    all_to_all x0 -> x2, waiting for transfers between devices: none -> 122 us  [body(): lax.all_to_all(jnp.stack([w_expert_in[expert]] * lax.axis_size('shard')),...]
    all_gather x1, blocking collectives: 31 us -> 128 us  [body(): lax.all_gather(w_router, 'shard', axis=0, tiled=True)]
    all_gather x2, waiting for transfers between devices: 143 us -> 93.6 us  [body(): lax.all_gather(w_expert_out[expert], 'shard', axis=0, tiled=True)]
    all_gather x1, waiting for transfers between devices: 46.1 us -> 0.01 us  [body(): lax.all_gather(w_proj, 'shard', axis=0, tiled=True)]
    all_gather x1, waiting for transfers between devices: 39.1 us -> 0.02 us  [body(): lax.all_gather(w_qkv, 'shard', axis=0, tiled=True)]
    all_to_all x0 -> x2, starting transfers between devices: none -> 27.2 us  [body(): lax.all_to_all(jnp.stack([w_expert_in[expert]] * lax.axis_size('shard')),...]
  transfers between devices with their start and end apart: 12 -> 12, of which waited for: 12 -> 9; matrix products, arithmetic and copies ran while one was open for 9% -> 9% of each run, Pallas kernels for 0% -> 0%
where the time goes in v1:
time: 1180 us; the launch traced here: 1170 us
  waiting for transfers between devices  789 us (67%)
  blocking collectives  202 us (17%)
  matrix products  80.7 us (7%)
  local copies, waits for them, and re-layouts  31.9 us (3%)
  starting transfers between devices  27.8 us (2%)
  other arithmetic  24 us (2%)
  between operations  15.4 us (1%)
    reduce_scatter x2, waiting for transfers between devices, body(): lax.psum_scatter(in_term(jnp.int32(0), shard_rows * lax.axis_size('shard'...  216 us
    reduce_scatter x2, waiting for transfers between devices, body(): lax.psum_scatter(out_term(jnp.int32(0), hid_rows * lax.axis_size('shard')...  159 us
    all_gather x1, blocking collectives, body(): lax.all_gather(w_router, 'shard', axis=0, tiled=True)  128 us
    all_to_all x2, waiting for transfers between devices, body(): lax.all_to_all(jnp.stack([w_expert_in[expert]] * lax.axis_size('shard')),...  122 us
    reduce_scatter x1, waiting for transfers between devices, body(): lax.psum_scatter(jnp.concatenate([jnp.einsum('rc,rk->ck', hidden1, grad_q...  108 us
    all_gather x2, waiting for transfers between devices, body(): lax.all_gather(w_expert_out[expert], 'shard', axis=0, tiled=True)  93.6 us
    psum x1, waiting for transfers between devices, body(): lax.psum(dense_local, 'rep').astype(jnp.float32)  88.8 us
    psum x1, blocking collectives, body(): gain1_total, gain2_total = lax.psum((gain1, gain2), ('shard', 'rep'))  74.5 us
  transfers between devices with their start and end apart: 12, of which 9 were waited for; matrix products, arithmetic and copies ran while one was open for 9% of the time, Pallas kernels for 0%

profile of v1, /device:TPU:24, one launch (start us, length us, event | category | flops | bytes accessed | tf_op | source)
XLA Modules:
  0.0 1171.6 jit_solution(16610136236871043938)
XLA Ops:
  12.5 11.5 all-to-all-start.1
  24.9 121.9 %all-to-all-done.1 = bf16[16,48,3072]{2,1,0:T(8,128)(2,1)} async-done(((bf16[16,48,3072]{2,1,0:T(8,128)(2,1)}), bf16[16,48,3072]{2,1,0:T(8,128)(2,1)}, u32[]{:S(2)}, u32[]{:S(2)}) %all-to-all-start.1) | async-done | bytes 4718624 | tf_op jit(solution)/shard_map/all_to_all | solution.py:150
  149.7 15.8 %all-to-all-start = ((bf16[16,48,3072]{2,1,0:T(8,128)(2,1)}), bf16[16,48,3072]{2,1,0:T(8,128)(2,1)}, u32[]{:S(2)}, u32[]{:S(2)}) async-start(bf16[16,48,3072]{2,1,0:T(8,128)(2,1)} %stack.48), calls=%async_computation | async-start | bytes 9437184 | tf_op jit(solution)/shard_map/all_to_all | solution.py:150
  167.8 127.9 %all-gather.2 = bf16[16,48,32]{1,2,0:T(8,128)(2,1)S(1)} all-gather(bf16[1,48,32]{1,2,0:T(8,128)(2,1)S(1)} %bitcast.187), channel_id=1, replica_groups=mesh['shard'=16,'rep'=16] {'shard'}, dimensions={0}, use_global_device_ids=true | all-gather | bytes 52224 | tf_op jit(solution)/shard_map/all_gather | solution.py:124
  314.7 7.6 fusion.26
  322.3 26.3 %all-gather.14.cloned.1.call-done = bf16[1,3072,768]{2,1,0:T(8,128)(2,1)} async-done(((bf16[1,192,768]{2,1,0:T(8,128)(2,1)}), bf16[1,3072,768]{2,1,0:T(8,128)(2,1)}) %all-gather.14.cloned.1.call-update) | async-done | bytes 4718608 | tf_op jit(solution)/shard_map/all_gather | solution.py:155
  348.6 4.0 fusion.61
  352.7 7.8 fusion.23
  360.5 67.3 %all-gather.12.cloned.1.call-done = bf16[1,3072,768]{2,1,0:T(8,128)(2,1)} async-done(((bf16[1,192,768]{2,1,0:T(8,128)(2,1)}), bf16[1,3072,768]{2,1,0:T(8,128)(2,1)}) %all-gather.12.cloned.1.call-update) | async-done | bytes 4718608 | tf_op jit(solution)/shard_map/all_gather | solution.py:155
  432.3 7.0 fusion.82
  441.4 3.7 convolution_convert_fusion
  445.1 4.8 convolution_convert_fusion.1
  450.0 4.8 fusion.14
  459.6 5.0 fusion.17
  471.4 4.3 fusion.60
  475.7 4.1 fusion.59
  499.3 49.8 %reduce-scatter.14.cloned.1.call-done = bf16[192,768]{1,0:T(8,128)(2,1)} async-done(((bf16[3072,768]{1,0:T(8,128)(2,1)}), bf16[192,768]{1,0:T(8,128)(2,1)}) %reduce-scatter.14.cloned.1.call-update) | async-done | bytes 294928 | tf_op jit(solution)/shard_map/reduce_scatter | solution.py:212
  549.1 109.0 %reduce-scatter.12.cloned.1.call-done = bf16[192,768]{1,0:T(8,128)(2,1)} async-done(((bf16[3072,768]{1,0:T(8,128)(2,1)}), bf16[192,768]{1,0:T(8,128)(2,1)}) %reduce-scatter.12.cloned.1.call-update) | async-done | bytes 294928 | tf_op jit(solution)/shard_map/reduce_scatter | solution.py:212
  660.0 106.6 %reduce-scatter.10.cloned.1.call-done = bf16[48,3072]{1,0:T(8,128)(2,1)} async-done(((bf16[768,3072]{1,0:T(8,128)(2,1)}), bf16[48,3072]{1,0:T(8,128)(2,1)}) %reduce-scatter.10.cloned.1.call-update) | async-done | bytes 294928 | tf_op jit(solution)/shard_map/reduce_scatter | solution.py:204
  766.7 109.1 %reduce-scatter.8.cloned.1.call-done = bf16[48,3072]{1,0:T(8,128)(2,1)} async-done(((bf16[768,3072]{1,0:T(8,128)(2,1)}), bf16[48,3072]{1,0:T(8,128)(2,1)}) %reduce-scatter.8.cloned.1.call-update) | async-done | bytes 294928 | tf_op jit(solution)/shard_map/reduce_scatter | solution.py:204
  877.7 108.5 %reduce-scatter.6.cloned.1.call-done = bf16[48,3104]{1,0:T(8,128)(2,1)} async-done(((bf16[768,3104]{1,0:T(8,128)(2,1)}), bf16[48,3104]{1,0:T(8,128)(2,1)}) %reduce-scatter.6.cloned.1.call-update) | async-done | bytes 298000 | tf_op jit(solution)/shard_map/reduce_scatter | solution.py:240
  986.3 4.2 fusion.78
  990.5 74.5 %all-reduce.1 = (f32[768]{0:T(1024)}, f32[768]{0:T(1024)}) all-reduce(f32[768]{0:T(1024)S(1)} %get-tuple-element.56, f32[768]{0:T(1024)S(1)} %get-tuple-element.54), channel_id=1, replica_groups=mesh['shard'=16,'rep'=16] {'shard','rep'}, use_global_device_ids=true, to_apply=%region_24.25 | all-reduce | flops 1536 | bytes 12288 | tf_op jit(solution)/shard_map/psum | solution.py:239
  1068.6 88.8 %all-reduce.5.cloned.1.call-done = (bf16[48,3104]{1,0:T(8,128)(2,1)}, bf16[2,48,3072]{2,1,0:T(8,128)(2,1)}, bf16[2,192,768]{2,1,0:T(8,128)(2,1)}) async-done(((bf16[48,3104]{1,0:T(8,128)(2,1)}, bf16[2,48,3072]{2,1,0:T(8,128)(2,1)}, bf16[2,192,768]{2,1,0:T(8,128)(2,1)}), (bf16[48,3104]{1,0:T(8,128)(2,1)}, bf16[2,48,3072]{2,1,0:T(8,128)(2,1)}, bf16[2,192,768]{2,1,0:T(8,128)(2,1)})) %all-reduce.5.cloned.1.call-update) | async-done | bytes 1477648 | tf_op jit(solution)/shard_map/psum | solution.py:254
  (221 shorter events, 81.9 us)
Async XLA Ops:
  7.2 290.7 %all-gather.8.cloned.1.call-start = ((), (), s32[]{:S(2)}) async-start(), calls=%async_computation.7 | async-start | bytes 3760128 | tf_op jit(solution)/shard_map/all_gather | solution.py:122
  7.9 298.6 %all-gather.10.cloned.1.call-start = ((), (), s32[]{:S(2)}) async-start(), calls=%async_computation.8 | async-start | bytes 1253376 | tf_op jit(solution)/shard_map/all_gather | solution.py:123
  12.5 134.3 %all-to-all-start.1 = ((bf16[16,48,3072]{2,1,0:T(8,128)(2,1)}), bf16[16,48,3072]{2,1,0:T(8,128)(2,1)}, u32[]{:S(2)}, u32[]{:S(2)}) async-start(bf16[16,48,3072]{2,1,0:T(8,128)(2,1)} %stack.50), calls=%async_computation.1 | async-start | bytes 9437184 | tf_op jit(solution)/shard_map/all_to_all | solution.py:150
  24.0 324.6 %all-gather.14.cloned.1.call-start = ((), (), s32[]{:S(2)}) async-start(), calls=%async_computation.15 | async-start | bytes 5013504 | tf_op jit(solution)/shard_map/all_gather | solution.py:155
  149.6 17.9 %copy-start.54 = (s32[2]{0:T(128)S(1)}, s32[2]{0:T(128)}, u32[]{:S(2)}) copy-start(s32[2]{0:T(128)} %param.20) | copy-start | bytes 28
  149.6 18.2 %copy-start.53 = (bf16[48,32]{0,1:T(8,128)(2,1)S(1)}, bf16[48,32]{0,1:T(8,128)(2,1)}, u32[]{:S(2)}) copy-start(bf16[48,32]{0,1:T(8,128)(2,1)} %param.16) | copy-start | bytes 9220
  149.7 146.9 %copy-start.3 = (bf16[197,768]{1,0:T(8,128)(2,1)S(1)}, bf16[197,768]{1,0:T(8,128)(2,1)}, u32[]{:S(2)}) copy-start(bf16[197,768]{1,0:T(8,128)(2,1)} %param.11) | copy-start | bytes 907780
  149.7 203.0 %all-to-all-start = ((bf16[16,48,3072]{2,1,0:T(8,128)(2,1)}), bf16[16,48,3072]{2,1,0:T(8,128)(2,1)}, u32[]{:S(2)}, u32[]{:S(2)}) async-start(bf16[16,48,3072]{2,1,0:T(8,128)(2,1)} %stack.48), calls=%async_computation | async-start | bytes 9437184 | tf_op jit(solution)/shard_map/all_to_all | solution.py:150
  165.4 132.4 %copy-start.46 = (f32[768]{0:T(1024)S(1)}, f32[768]{0:T(1024)}, u32[]{:S(2)}) copy-start(f32[768]{0:T(1024)} %param.12) | copy-start | bytes 9220
  165.4 262.4 %all-gather.12.cloned.1.call-start = ((), (), s32[]{:S(2)}) async-start(), calls=%async_computation.14 | async-start | bytes 5013504 | tf_op jit(solution)/shard_map/all_gather | solution.py:155
  166.0 383.1 %reduce-scatter.14.cloned.1.call-start = ((), (), s32[]{:S(2)}) async-start(), calls=%async_computation.13 | async-start | bytes 5013504 | tf_op jit(solution)/shard_map/reduce_scatter | solution.py:212
  167.8 133.0 %copy-start.20 = (f32[197,2,2]{2,1,0:T(2,128)}, f32[197,2,2]{2,1,0:T(2,128)S(1)}, u32[]{:S(2)}) copy-start(f32[197,2,2]{2,1,0:T(2,128)S(1)} %copy.110) | copy-start | bytes 9460
  445.0 213.1 %reduce-scatter.12.cloned.1.call-start = ((), (), s32[]{:S(2)}) async-start(), calls=%async_computation.12 | async-start | bytes 5013504 | tf_op jit(solution)/shard_map/reduce_scatter | solution.py:212
  449.9 316.7 %reduce-scatter.10.cloned.1.call-start = ((), (), s32[]{:S(2)}) async-start(), calls=%async_computation.11 | async-start | bytes 5013504 | tf_op jit(solution)/shard_map/reduce_scatter | solution.py:204
  459.3 416.5 %reduce-scatter.8.cloned.1.call-start = ((), (), s32[]{:S(2)}) async-start(), calls=%async_computation.10 | async-start | bytes 5013504 | tf_op jit(solution)/shard_map/reduce_scatter | solution.py:204
  469.0 517.2 %reduce-scatter.6.cloned.1.call-start = ((), (), s32[]{:S(2)}) async-start(), calls=%async_computation.9 | async-start | bytes 5222400 | tf_op jit(solution)/shard_map/reduce_scatter | solution.py:240
  499.3 658.1 %all-reduce.5.cloned.1.call-start = ((), (), s32[]{:S(2)}) async-start(), calls=%async_computation.16 | async-start | bytes 2973696 | tf_op jit(solution)/shard_map/psum | solution.py:254
  660.0 326.2 %copy-start.39 = (bf16[12,64,197]{2,1,0:T(8,128)(2,1)S(1)}, bf16[12,64,197]{2,1,0:T(8,128)(2,1)}, u32[]{:S(2)}) copy-start(bf16[12,64,197]{2,1,0:T(8,128)(2,1)} %copy-done.38) | copy-start | bytes 907780
  660.0 326.2 %copy-start.41 = (bf16[12,64,197]{2,1,0:T(8,128)(2,1)S(1)}, bf16[12,64,197]{2,1,0:T(8,128)(2,1)}, u32[]{:S(2)}) copy-start(bf16[12,64,197]{2,1,0:T(8,128)(2,1)} %copy-done.40) | copy-start | bytes 907780
  660.0 326.2 %copy-start.43 = (bf16[12,64,197]{2,1,0:T(8,128)(2,1)S(1)}, bf16[12,64,197]{2,1,0:T(8,128)(2,1)}, u32[]{:S(2)}) copy-start(bf16[12,64,197]{2,1,0:T(8,128)(2,1)} %copy-done.42) | copy-start | bytes 907780
  986.3 80.1 %copy-start.19 = (f32[197,2,128]{2,1,0:T(2,128)S(1)}, f32[197,2,128]{2,1,0:T(2,128)}, u32[]{:S(2)}) copy-start(f32[197,2,128]{2,1,0:T(2,128)} %copy-done.18) | copy-start | bytes 605188
  986.3 80.1 %copy-start.28 = (bf16[1,128,768]{2,1,0:T(8,128)(2,1)S(1)}, bf16[1,128,768]{2,1,0:T(8,128)(2,1)}, u32[]{:S(2)}) copy-start(bf16[1,128,768]{2,1,0:T(8,128)(2,1)} %fusion.61) | copy-start | bytes 589828
  986.3 80.1 %copy-start.30 = (bf16[1,128,768]{2,1,0:T(8,128)(2,1)S(1)}, bf16[1,128,768]{2,1,0:T(8,128)(2,1)}, u32[]{:S(2)}) copy-start(bf16[1,128,768]{2,1,0:T(8,128)(2,1)} %copy-done.29) | copy-start | bytes 589828
  990.4 77.0 %copy-start.2 = (f32[197,768]{1,0:T(8,128)S(1)}, f32[197,768]{1,0:T(8,128)}, u32[]{:S(2)}) copy-start(f32[197,768]{1,0:T(8,128)} %copy-done) | copy-start | bytes 1815556
  (43 other events, 140.3 us)
Sparse Core Ops, SparseCore 0:
  10.7 102.4 all-gather.7
  115.9 106.8 all-gather.9
  226.0 122.5 all-gather.13
  351.2 76.5 all-gather.11
  445.2 103.9 reduce-scatter.13
  554.0 104.0 reduce-scatter.11
  662.5 104.1 reduce-scatter.9
  771.6 104.1 reduce-scatter.7
  880.3 105.8 reduce-scatter.5
  990.1 167.2 all-reduce.4
